TPU v7x, 256 devices: a whole 4x4x8 slice. The times are simulated.
256 devices in a mesh: hi: 16 (over z, core), lo: 16 (over x, y).
Axes of the slice: x: 4, y: 4, z: 8, core: 2. Of those that a mesh axis runs over, the one named last changes fastest.
Arguments:
- points: float32 [3, 1024, 512], P(None, ('hi', 'lo')), as said below
- solution: float32 [16, 1024, 512], P(None, ('hi', 'lo')), may hold values from -6 to 6
- residual: float32 [16, 1024, 512], P(None, ('hi', 'lo')), may hold values from -300 to 300
- direction: float32 [16, 1024, 512], P(None, ('hi', 'lo')), may hold values from -300 to 300
- nugget: float32 [1024, 512], P(('hi', 'lo')), may hold values from 0.5 to 2
- leaf_basis: float32 [1024, 512, 128], P(('hi', 'lo')), may hold values from -0.25 to 0.25
- transfer: float32 [1024, 128, 128], P(('hi', 'lo')), may hold values from -0.5 to 0.5
- far_coupling: float32 [1024, 16, 128, 128], P(('hi', 'lo')), may hold values from -0.125 to 0.125
- coarse_up: float32 [256, 8, 128, 128], P(('hi', 'lo')), may hold values from -0.5 to 0.5
- coarse_down: float32 [256, 8, 128, 128], P(('hi', 'lo')), may hold values from -0.5 to 0.5
- near_ids: int32 [1024, 27], P(('hi', 'lo')), may hold values from 0 to 1023, as said below
- near_count: int32 [1024], P(('hi', 'lo')), may hold values from 1 to 27, as said below
- far_ids: int32 [1024, 16], P(('hi', 'lo')), may hold values from 0 to 1023, as said below
Outputs:
- new_solution: float32 [16, 1024, 512], P(None, ('hi', 'lo'))
- new_residual: float32 [16, 1024, 512], P(None, ('hi', 'lo'))
- new_direction: float32 [16, 1024, 512], P(None, ('hi', 'lo'))
Inputs may be any that keep to these rules, and one draw needn't show every extreme that they name: The points of leaf i lie in the cube of side 3 centred on the unit Morton cell of i, that cell read from the bits of i in x, y, z order from the lowest bit. `near_ids`: row i starts with i itself; every entry of row i lies in the aligned block of 64 leaves that holds i; entries from slot near_count[i] on are not used. `near_count`: some leaf uses all 27 slots. `far_ids`: every entry of row i lies in the aligned block of 64 leaves that holds i.
All inputs are finite; a program needn't handle non-finite values.
Results may differ from a plain program's by a relative error of at most 0.0003.
Values sent between devices are 32-bit elements; how exact they have to be, the bound alone decides.
A program may use at most 128 MiB of HBM per device.

v0:
```python
import math

import jax
import jax.numpy as jnp
from jax import lax
from jax.sharding import PartitionSpec as P

length_scale = 1.0
root_three = math.sqrt(3.0)
epsilon = 1e-06
highest = lax.Precision.HIGHEST


def partner(array, axis, apart):
    return lax.ppermute(array, axis, [(i, i ^ 1 << apart) for i in range(lax.axis_size(axis))])


def matern_block(target_points, source_points):
    squared = jnp.zeros(
        (target_points.shape[1], target_points.shape[2], source_points.shape[2]), jnp.float32
    )
    for coord in range(3):
        gap = target_points[coord][:, :, None] - source_points[coord][:, None, :]
        squared = squared + gap * gap
    scaled = root_three / length_scale * jnp.sqrt(squared)
    return (1.0 + scaled) * jnp.exp(-scaled)


def block_product(target_points, source_leaves, group_points, group_values):
    source_points = jnp.take(group_points, source_leaves, axis=1)
    kernel = matern_block(target_points, source_points)
    values = jnp.take(group_values, source_leaves, axis=1)
    return jnp.einsum("lab,nlb->nla", kernel, values, precision=highest)


def per_device(
    points,
    solution,
    residual,
    direction,
    nugget,
    leaf_basis,
    transfer,
    far_coupling,
    coarse_up,
    coarse_down,
    near_ids,
    near_count,
    far_ids,
):
    leaf_count = points.shape[1]
    probe_count = direction.shape[0]
    leaf_width = points.shape[2]
    rank_width = leaf_basis.shape[2]
    far_count = far_ids.shape[1]
    group_size = lax.axis_size("lo")
    group_width = leaf_count * group_size
    group_start = lax.axis_index("hi") * group_width
    coefficients = jnp.einsum("nla,lar->nlr", direction, leaf_basis, precision=highest)
    local_square = jnp.sum(residual * residual, axis=(1, 2))
    start = lax.psum(local_square, ("hi", "lo"))
    group_points, group_values, group_coeff = (
        lax.all_gather(points, "lo", axis=1, tiled=True),
        lax.all_gather(direction, "lo", axis=1, tiled=True),
        lax.all_gather(coefficients, "lo", axis=1, tiled=True),
    )
    own_sources = near_ids - group_start
    turns = jnp.max(near_count)

    def near_turn(slot_index, total):
        source_leaves = lax.dynamic_index_in_dim(own_sources, slot_index, 1, keepdims=False)
        keep_mask = (slot_index < near_count).astype(jnp.float32)
        part_sum = block_product(points, source_leaves, group_points, group_values)
        return total + part_sum * keep_mask[None, :, None]

    near = lax.fori_loop(
        0, turns, near_turn, jnp.zeros((probe_count, leaf_count, leaf_width), jnp.float32)
    )
    near = near + nugget[None] * direction
    far_positions = (far_ids - group_start).reshape(-1)
    far_coeff = jnp.take(group_coeff, far_positions, axis=1).reshape(
        probe_count, leaf_count, far_count, rank_width
    )
    local_coeff = jnp.einsum("nlfq,lfqr->nlr", far_coeff, far_coupling, precision=highest)
    box = jnp.einsum("nlq,lqr->nr", coefficients, transfer, precision=highest)
    level = jnp.einsum("nq,kqr->knr", box, coarse_up[0], precision=highest)
    box_total = lax.axis_size(("hi", "lo"))
    level_count = box_total.bit_length() - 1
    pending = level
    collected = []
    for depth in range(level_count):
        received = partner(pending, ("hi", "lo"), depth)
        collected.append(received[0])
        pending = (pending + received)[1:]
    sibling = jnp.stack(collected, axis=0)
    level_scale = 2.0 ** (-0.5 * jnp.arange(level_count, dtype=jnp.float32))
    down = jnp.einsum(
        "knr,krq->nq", sibling * level_scale[:, None, None], coarse_down[0], precision=highest
    )
    local_coeff = local_coeff + jnp.einsum("nq,lrq->nlr", down, transfer, precision=highest)
    image = near + jnp.einsum("nlr,lar->nla", local_coeff, leaf_basis, precision=highest)
    local_curvature = jnp.sum(direction * image, axis=(1, 2))
    curvature = lax.psum(local_curvature, ("hi", "lo"))
    alpha = start / curvature
    new_residual = residual - alpha[:, None, None] * image
    finish = lax.psum(jnp.sum(new_residual * new_residual, axis=(1, 2)), ("hi", "lo"))
    new_solution = solution + alpha[:, None, None] * direction
    new_direction = new_residual + (finish / (start + epsilon))[:, None, None] * direction
    return (new_solution, new_residual, new_direction)


def solution(mesh):
    placed = (
        P(None, ("hi", "lo"), None),
        P(None, ("hi", "lo"), None),
        P(None, ("hi", "lo"), None),
        P(None, ("hi", "lo"), None),
        P(("hi", "lo"), None),
        P(("hi", "lo"), None, None),
        P(("hi", "lo"), None, None),
        P(("hi", "lo"), None, None, None),
        P(("hi", "lo"), None, None, None),
        P(("hi", "lo"), None, None, None),
        P(("hi", "lo"), None),
        P(("hi", "lo")),
        P(("hi", "lo"), None),
    )
    return jax.shard_map(
        per_device,
        mesh=mesh,
        in_specs=placed,
        out_specs=(
            P(None, ("hi", "lo"), None),
            P(None, ("hi", "lo"), None),
            P(None, ("hi", "lo"), None),
        ),
        check_vma=False,
    )
```

profile of v0, /device:TPU:1, one launch (start us, length us, event | category | flops | bytes accessed | tf_op | source)
XLA Modules:
  0.0 539.8 jit_solution(7370283211513614932)
XLA Ops:
  7.2 1.2 copy-done
  8.4 1.6 convolution_bitcast_fusion.3
  10.0 1.2 fusion.52
  11.2 1.4 convolution_bitcast_fusion.1
  12.6 2.2 collective-permute-start
  14.8 1.6 copy.46
  16.5 19.4 %all_gather.11 = f32[16,64,128]{2,0,1:T(8,128)S(1)} all-gather(f32[16,4,128]{2,0,1:T(8,128)S(1)} %convolution_bitcast_fusion.3), channel_id=1, replica_groups=mesh['hi'=16,'lo'=16] {'lo'}, dimensions={1}, use_global_device_ids=true | all-gather | bytes 557056 | tf_op jit(solution)/shard_map/all_gather | solution.py:65
  35.8 0.7 compare_and_fusion
  36.6 0.8 copy.41
  37.4 0.8 copy.43
  38.2 1.1 multiply_reduce_fusion.2
  39.3 0.6 gather_fusion.2
  39.9 4.0 convolution_bitcast_fusion.2
  44.0 2.0 collective-permute-start.1
  45.9 2.6 collective-permute-done.1
  48.7 2.9 collective-permute-done.2
  51.6 1.1 collective-permute-start.3
  52.7 3.3 collective-permute-done.3
  56.0 10.9 %collective-permute-start.4 = (f32[4,16,128]{2,1,0:T(8,128)S(1)}, f32[4,16,128]{2,1,0:T(8,128)S(1)}, u32[]{:S(2)}, u32[]{:S(2)}) collective-permute-start(f32[4,16,128]{2,1,0:T(8,128)S(1)} %slice_add_fusion.3), channel_id=1, source_target_pairs={{0,16},{1,17},{2,18},{3,19},{4,20},{5,21},{6,22},{7,23},{8,24},{9,... | collective-permute-start | bytes 98312 | tf_op jit(solution)/shard_map/ppermute | solution.py:15
  66.9 0.9 collective-permute-done.4
  67.7 1.3 collective-permute-start.5
  69.0 1.4 collective-permute-done.5
  70.4 2.3 collective-permute-start.6
  72.7 1.2 collective-permute-done.6
  73.9 6.0 %collective-permute-start.7 = (f32[1,16,128]{2,1,0:T(8,128)S(1)}, f32[1,16,128]{2,1,0:T(8,128)S(1)}, u32[]{:S(2)}, u32[]{:S(2)}) collective-permute-start(f32[1,16,128]{2,1,0:T(8,128)S(1)} %get-tuple-element.91), channel_id=1, source_target_pairs={{0,128},{1,129},{2,130},{3,131},{4,132},{5,133},{6,134},{7,135},{8... | collective-permute-start | bytes 24584 | tf_op jit(solution)/shard_map/ppermute | solution.py:15
  80.0 17.3 %all_gather.10 = f32[3,64,512]{2,0,1:T(4,128)S(1)} all-gather(f32[3,4,512]{2,0,1:T(4,128)S(1)} %copy.43), channel_id=1, replica_groups=mesh['hi'=16,'lo'=16] {'lo'}, dimensions={1}, use_global_device_ids=true | all-gather | bytes 417792 | tf_op jit(solution)/shard_map/all_gather | solution.py:63
  97.3 0.6 reduce_max.9
  98.7 124.9 %while.10 = (s32[]{:T(128)}, f32[16,4,512]{2,0,1:T(8,128)S(1)}, s32[]{:T(128)}, s32[4,27]{0,1:T(8,128)S(1)}, f32[16,64,512]{2,0,1:T(8,128)}, /*index=5*/f32[3,4,...) while((s32[]{:T(128)}, f32[16,4,512]{2,0,1:T(8,128)S(1)}, ...), condition=%wide.region_4.5_spmd, body=%wide.region_3.4_spmd.sunk | while | flops 214015008 | bytes 954659 | solution.py:76
  99.5 0.6 gather_fusion
  100.2 2.1 gather_fusion.1
  102.4 6.8 %fusion.69 = f32[16,4,512]{2,0,1:T(8,128)S(1)} fusion(f32[16,4,512]{2,0,1:T(8,128)S(1)} %get-tuple-element.179, f32[4,512]{1,0:T(4,128)S(1)} %get-tuple-element.160, f32[4,512]{1,0:T(4,128)S(1)} %get-tuple-element.162, f32[4,512]{1,0:T(4,128)S(1)} %get-tuple-element.163, f32[4,512]{1,0:T(4,128)S(1)} %get-tuple-element.164, ...), kind=kOutput, calls=%fused_computation.28.clone.1 | convolution fusion | flops 214007808 | bytes 442388 | tf_op jit(solution)/shard_map/while/body/lab,nlb->nla/dot_general | solution.py:33
  109.8 0.6 gather_fusion
  110.5 2.1 gather_fusion.1
  112.7 6.8 %fusion.69 = f32[16,4,512]{2,0,1:T(8,128)S(1)} fusion(f32[16,4,512]{2,0,1:T(8,128)S(1)} %get-tuple-element.179, f32[4,512]{1,0:T(4,128)S(1)} %get-tuple-element.160, f32[4,512]{1,0:T(4,128)S(1)} %get-tuple-element.162, f32[4,512]{1,0:T(4,128)S(1)} %get-tuple-element.163, f32[4,512]{1,0:T(4,128)S(1)} %get-tuple-element.164, ...), kind=kOutput, calls=%fused_computation.28.clone.1 | convolution fusion | flops 214007808 | bytes 442388 | tf_op jit(solution)/shard_map/while/body/lab,nlb->nla/dot_general | solution.py:33
  120.2 0.6 gather_fusion
  120.9 2.1 gather_fusion.1
  123.1 6.8 %fusion.69 = f32[16,4,512]{2,0,1:T(8,128)S(1)} fusion(f32[16,4,512]{2,0,1:T(8,128)S(1)} %get-tuple-element.179, f32[4,512]{1,0:T(4,128)S(1)} %get-tuple-element.160, f32[4,512]{1,0:T(4,128)S(1)} %get-tuple-element.162, f32[4,512]{1,0:T(4,128)S(1)} %get-tuple-element.163, f32[4,512]{1,0:T(4,128)S(1)} %get-tuple-element.164, ...), kind=kOutput, calls=%fused_computation.28.clone.1 | convolution fusion | flops 214007808 | bytes 442388 | tf_op jit(solution)/shard_map/while/body/lab,nlb->nla/dot_general | solution.py:33
  130.5 0.6 gather_fusion
  131.2 2.1 gather_fusion.1
  133.4 6.8 %fusion.69 = f32[16,4,512]{2,0,1:T(8,128)S(1)} fusion(f32[16,4,512]{2,0,1:T(8,128)S(1)} %get-tuple-element.179, f32[4,512]{1,0:T(4,128)S(1)} %get-tuple-element.160, f32[4,512]{1,0:T(4,128)S(1)} %get-tuple-element.162, f32[4,512]{1,0:T(4,128)S(1)} %get-tuple-element.163, f32[4,512]{1,0:T(4,128)S(1)} %get-tuple-element.164, ...), kind=kOutput, calls=%fused_computation.28.clone.1 | convolution fusion | flops 214007808 | bytes 442388 | tf_op jit(solution)/shard_map/while/body/lab,nlb->nla/dot_general | solution.py:33
  140.9 0.6 gather_fusion
  141.6 2.1 gather_fusion.1
  143.8 6.8 %fusion.69 = f32[16,4,512]{2,0,1:T(8,128)S(1)} fusion(f32[16,4,512]{2,0,1:T(8,128)S(1)} %get-tuple-element.179, f32[4,512]{1,0:T(4,128)S(1)} %get-tuple-element.160, f32[4,512]{1,0:T(4,128)S(1)} %get-tuple-element.162, f32[4,512]{1,0:T(4,128)S(1)} %get-tuple-element.163, f32[4,512]{1,0:T(4,128)S(1)} %get-tuple-element.164, ...), kind=kOutput, calls=%fused_computation.28.clone.1 | convolution fusion | flops 214007808 | bytes 442388 | tf_op jit(solution)/shard_map/while/body/lab,nlb->nla/dot_general | solution.py:33
  151.2 0.6 gather_fusion
  151.9 2.1 gather_fusion.1
  154.1 6.8 %fusion.69 = f32[16,4,512]{2,0,1:T(8,128)S(1)} fusion(f32[16,4,512]{2,0,1:T(8,128)S(1)} %get-tuple-element.179, f32[4,512]{1,0:T(4,128)S(1)} %get-tuple-element.160, f32[4,512]{1,0:T(4,128)S(1)} %get-tuple-element.162, f32[4,512]{1,0:T(4,128)S(1)} %get-tuple-element.163, f32[4,512]{1,0:T(4,128)S(1)} %get-tuple-element.164, ...), kind=kOutput, calls=%fused_computation.28.clone.1 | convolution fusion | flops 214007808 | bytes 442388 | tf_op jit(solution)/shard_map/while/body/lab,nlb->nla/dot_general | solution.py:33
  162.3 2.1 gather_fusion.1
  164.4 6.8 %fusion.69 = f32[16,4,512]{2,0,1:T(8,128)S(1)} fusion(f32[16,4,512]{2,0,1:T(8,128)S(1)} %get-tuple-element.179, f32[4,512]{1,0:T(4,128)S(1)} %get-tuple-element.160, f32[4,512]{1,0:T(4,128)S(1)} %get-tuple-element.162, f32[4,512]{1,0:T(4,128)S(1)} %get-tuple-element.163, f32[4,512]{1,0:T(4,128)S(1)} %get-tuple-element.164, ...), kind=kOutput, calls=%fused_computation.28.clone.1 | convolution fusion | flops 214007808 | bytes 442388 | tf_op jit(solution)/shard_map/while/body/lab,nlb->nla/dot_general | solution.py:33
  172.6 2.1 gather_fusion.1
  174.8 6.8 %fusion.69 = f32[16,4,512]{2,0,1:T(8,128)S(1)} fusion(f32[16,4,512]{2,0,1:T(8,128)S(1)} %get-tuple-element.179, f32[4,512]{1,0:T(4,128)S(1)} %get-tuple-element.160, f32[4,512]{1,0:T(4,128)S(1)} %get-tuple-element.162, f32[4,512]{1,0:T(4,128)S(1)} %get-tuple-element.163, f32[4,512]{1,0:T(4,128)S(1)} %get-tuple-element.164, ...), kind=kOutput, calls=%fused_computation.28.clone.1 | convolution fusion | flops 214007808 | bytes 442388 | tf_op jit(solution)/shard_map/while/body/lab,nlb->nla/dot_general | solution.py:33
  183.0 2.1 gather_fusion.1
  185.1 6.8 %fusion.69 = f32[16,4,512]{2,0,1:T(8,128)S(1)} fusion(f32[16,4,512]{2,0,1:T(8,128)S(1)} %get-tuple-element.179, f32[4,512]{1,0:T(4,128)S(1)} %get-tuple-element.160, f32[4,512]{1,0:T(4,128)S(1)} %get-tuple-element.162, f32[4,512]{1,0:T(4,128)S(1)} %get-tuple-element.163, f32[4,512]{1,0:T(4,128)S(1)} %get-tuple-element.164, ...), kind=kOutput, calls=%fused_computation.28.clone.1 | convolution fusion | flops 214007808 | bytes 442388 | tf_op jit(solution)/shard_map/while/body/lab,nlb->nla/dot_general | solution.py:33
  193.3 2.1 gather_fusion.1
  195.5 6.8 %fusion.69 = f32[16,4,512]{2,0,1:T(8,128)S(1)} fusion(f32[16,4,512]{2,0,1:T(8,128)S(1)} %get-tuple-element.179, f32[4,512]{1,0:T(4,128)S(1)} %get-tuple-element.160, f32[4,512]{1,0:T(4,128)S(1)} %get-tuple-element.162, f32[4,512]{1,0:T(4,128)S(1)} %get-tuple-element.163, f32[4,512]{1,0:T(4,128)S(1)} %get-tuple-element.164, ...), kind=kOutput, calls=%fused_computation.28.clone.1 | convolution fusion | flops 214007808 | bytes 442388 | tf_op jit(solution)/shard_map/while/body/lab,nlb->nla/dot_general | solution.py:33
  203.7 2.1 gather_fusion.1
  205.8 6.8 %fusion.69 = f32[16,4,512]{2,0,1:T(8,128)S(1)} fusion(f32[16,4,512]{2,0,1:T(8,128)S(1)} %get-tuple-element.179, f32[4,512]{1,0:T(4,128)S(1)} %get-tuple-element.160, f32[4,512]{1,0:T(4,128)S(1)} %get-tuple-element.162, f32[4,512]{1,0:T(4,128)S(1)} %get-tuple-element.163, f32[4,512]{1,0:T(4,128)S(1)} %get-tuple-element.164, ...), kind=kOutput, calls=%fused_computation.28.clone.1 | convolution fusion | flops 214007808 | bytes 442388 | tf_op jit(solution)/shard_map/while/body/lab,nlb->nla/dot_general | solution.py:33
  214.0 2.1 gather_fusion.1
  216.2 6.8 %fusion.69 = f32[16,4,512]{2,0,1:T(8,128)S(1)} fusion(f32[16,4,512]{2,0,1:T(8,128)S(1)} %get-tuple-element.179, f32[4,512]{1,0:T(4,128)S(1)} %get-tuple-element.160, f32[4,512]{1,0:T(4,128)S(1)} %get-tuple-element.162, f32[4,512]{1,0:T(4,128)S(1)} %get-tuple-element.163, f32[4,512]{1,0:T(4,128)S(1)} %get-tuple-element.164, ...), kind=kOutput, calls=%fused_computation.28.clone.1 | convolution fusion | flops 214007808 | bytes 442388 | tf_op jit(solution)/shard_map/while/body/lab,nlb->nla/dot_general | solution.py:33
  223.6 1.1 multiply_reduce_fusion.1
  224.7 231.1 %all-reduce = (f32[16]{0:T(128)S(1)}, f32[16]{0:T(128)S(1)}) all-reduce(f32[16]{0:T(128)S(1)} %multiply_reduce_fusion.2, f32[16]{0:T(128)S(1)} %get-tuple-element.93), channel_id=1, replica_groups=mesh['hi'=16,'lo'=16] {'hi','lo'}, use_global_device_ids=true, to_apply=%region_1.0 | all-reduce | flops 32 | bytes 256 | tf_op jit(solution)/shard_map/psum | solution.py:61
  456.0 74.5 %psum.23 = f32[16]{0:T(128)S(1)} all-reduce(f32[16]{0:T(128)S(1)} %get-tuple-element.76), channel_id=1, replica_groups=mesh['hi'=16,'lo'=16] {'hi','lo'}, use_global_device_ids=true, to_apply=%region_8.9 | all-reduce | flops 16 | bytes 128 | tf_op jit(solution)/shard_map/psum | solution.py:106
  530.6 0.7 copy.52
  531.4 0.7 copy.51
  532.2 0.7 copy.53
  (139 shorter events, 6.5 us)
Async XLA Ops:
  7.2 1.2 copy-start
  7.2 91.5 %all-gather.2.cloned.1.call-start = ((), (), s32[]{:S(2)}) async-start(), calls=%async_computation | async-start | bytes 2228224 | tf_op jit(solution)/shard_map/all_gather | solution.py:64
  12.6 84.7 %copy-start.8 = (s32[4]{0:T(128)S(1)}, s32[4]{0:T(128)}, u32[]{:S(2)}) copy-start(s32[4]{0:T(128)} %param.26) | copy-start | bytes 52
  12.6 85.3 %copy-start.5 = (f32[1,8,128,128]{3,2,1,0:T(8,128)S(1)}, f32[1,8,128,128]{3,2,1,0:T(8,128)}, u32[]{:S(2)}) copy-start(f32[1,8,128,128]{3,2,1,0:T(8,128)} %param.24) | copy-start | bytes 1572868
  12.6 31.3 %collective-permute-start = (f32[8,16,128]{2,1,0:T(8,128)S(1)}, f32[8,16,128]{2,1,0:T(8,128)S(1)}, u32[]{:S(2)}, u32[]{:S(2)}) collective-permute-start(f32[8,16,128]{2,1,0:T(8,128)S(1)} %convolution_bitcast_fusion.1), channel_id=1, source_target_pairs={{0,1},{1,0},{2,3},{3,2},{4,5},{5,4},{6,7},{7,6},{8,9},{9,8},{10,11... | collective-permute-start | bytes 196616 | tf_op jit(solution)/shard_map/ppermute | solution.py:15
  16.5 81.8 %copy-start.2 = (f32[4,128,128]{2,1,0:T(8,128)S(1)}, f32[4,128,128]{2,1,0:T(8,128)}, u32[]{:S(2)}) copy-start(f32[4,128,128]{2,1,0:T(8,128)} %param.21) | copy-start | bytes 786436
  38.2 60.5 %copy-start.3 = (f32[3,4,512]{2,1,0:T(4,128)S(1)}, f32[3,4,512]{2,1,0:T(4,128)}, u32[]{:S(2)}) copy-start(f32[3,4,512]{2,1,0:T(4,128)} %param.15) | copy-start | bytes 73732
  44.0 4.6 collective-permute-start.1
  48.6 3.0 collective-permute-start.2
  51.6 4.4 collective-permute-start.3
  56.0 11.8 %collective-permute-start.4 = (f32[4,16,128]{2,1,0:T(8,128)S(1)}, f32[4,16,128]{2,1,0:T(8,128)S(1)}, u32[]{:S(2)}, u32[]{:S(2)}) collective-permute-start(f32[4,16,128]{2,1,0:T(8,128)S(1)} %slice_add_fusion.3), channel_id=1, source_target_pairs={{0,16},{1,17},{2,18},{3,19},{4,20},{5,21},{6,22},{7,23},{8,24},{9,... | collective-permute-start | bytes 98312 | tf_op jit(solution)/shard_map/ppermute | solution.py:15
  67.7 2.7 collective-permute-start.5
  70.4 3.5 collective-permute-start.6
  73.9 24.0 %collective-permute-start.7 = (f32[1,16,128]{2,1,0:T(8,128)S(1)}, f32[1,16,128]{2,1,0:T(8,128)S(1)}, u32[]{:S(2)}, u32[]{:S(2)}) collective-permute-start(f32[1,16,128]{2,1,0:T(8,128)S(1)} %get-tuple-element.91), channel_id=1, source_target_pairs={{0,128},{1,129},{2,130},{3,131},{4,132},{5,133},{6,134},{7,135},{8... | collective-permute-start | bytes 24584 | tf_op jit(solution)/shard_map/ppermute | solution.py:15
  98.7 124.9 %copy-start.1 = (f32[16,4,512]{2,1,0:T(4,128)S(1)}, f32[16,4,512]{2,1,0:T(4,128)}, u32[]{:S(2)}) copy-start(f32[16,4,512]{2,1,0:T(4,128)} %param.18) | copy-start | bytes 393220
  98.7 124.9 %copy-start.7 = (f32[4,512]{1,0:T(4,128)S(1)}, f32[4,512]{1,0:T(4,128)}, u32[]{:S(2)}) copy-start(f32[4,512]{1,0:T(4,128)} %param.19) | copy-start | bytes 24580
  98.7 357.1 %copy-start.4 = (f32[16,4,512]{2,1,0:T(4,128)S(1)}, f32[16,4,512]{2,1,0:T(4,128)}, u32[]{:S(2)}) copy-start(f32[16,4,512]{2,1,0:T(4,128)} %param.17) | copy-start | bytes 393220
  98.7 432.6 %copy-start.6 = (f32[16,4,512]{2,1,0:T(4,128)S(1)}, f32[16,4,512]{2,1,0:T(4,128)}, u32[]{:S(2)}) copy-start(f32[16,4,512]{2,1,0:T(4,128)} %param.16) | copy-start | bytes 393220
Sparse Core Ops, SparseCore 0:
  16.6 51.8 all-gather.1
where the time goes:
time: 541 us; the launch traced here: 540 us
  blocking collectives  342 us (63%)
  matrix products  91.1 us (17%)
  local copies, waits for them, and re-layouts  40.4 us (7%)
  starting transfers between devices  25.8 us (5%)
  between operations  14.3 us (3%)
  waiting for transfers between devices  12.4 us (2%)
  loops' own time  9.41 us (2%)
    psum x1, blocking collectives, per_device(): start = lax.psum(local_square, ('hi', 'lo'))  231 us
    dot_general x12, matrix products, block_product(): return jnp.einsum('lab,nlb->nla', kernel, values, precision=highest)  81.2 us
    psum x1, blocking collectives, per_device(): lax.psum(jnp.sum(new_residual * new_residual, axis=(1, 2)), ('hi', 'lo'))  74.5 us
    ppermute x8, starting transfers between devices, partner(): lax.ppermute(array, axis, [(i, i ^ 1 << apart) for i in range(lax.axis_si...  25.8 us
    gather x12, local copies, waits for them, and re-layouts, block_product(): values = jnp.take(group_values, source_leaves, axis=1)  25.7 us
    all_gather x1, blocking collectives, per_device(): lax.all_gather(coefficients, 'lo', axis=1, tiled=True)  19.4 us
    all_gather x1, blocking collectives, per_device(): lax.all_gather(points, 'lo', axis=1, tiled=True)  17.3 us
    ppermute x8, waiting for transfers between devices, partner(): lax.ppermute(array, axis, [(i, i ^ 1 << apart) for i in range(lax.axis_si...  12.3 us
  transfers between devices with their start and end apart: 9, of which 6 were waited for; matrix products, arithmetic and copies ran while one was open for 2% of the time, Pallas kernels for 0%

commit v1 on v0

v1 whole, which is shorter than its diff:
```python
import functools
import math

import jax
import jax.numpy as jnp
from jax import lax
from jax.experimental import pallas as pl
from jax.experimental.pallas import tpu as pltpu
from jax.sharding import PartitionSpec as P

epsilon = 1e-06
ln2 = math.log(2.0)
log2e = 1.0 / ln2
point_scale = math.sqrt(3.0) * log2e
f32, bf16 = jnp.float32, jnp.bfloat16
MESH = pl.DeviceIdType.MESH
VMEM = pl.BlockSpec(memory_space=pltpu.VMEM)
SMEM = pl.BlockSpec(memory_space=pltpu.SMEM)
ANY = pl.BlockSpec(memory_space=pl.ANY)

LEAF, RANK, PROBES, NEAR, FAR, OWN, LEVELS = 512, 128, 16, 27, 16, 4, 8
SIDE, DEPTH = 4, 8
ROWS = 24
GROUP = OWN * SIDE * SIDE
PEERS = SIDE * SIDE


def split(value):
    high = value.astype(bf16)
    return high, (value - high.astype(f32)).astype(bf16)


def dot3(left, right, dims):
    (lh, ll), (rh, rl) = split(left), split(right)
    dot = functools.partial(lax.dot_general, dimension_numbers=(dims, ((), ())), preferred_element_type=f32)
    return dot(lh, rh) + (dot(ll, rh) + dot(lh, rl))


NN, NT = ((1,), (0,)), ((1,), (1,))


def exchange_kernel(packet, level, gathered, sibling, pending, arrived, send, receive, own_sem, tree_send, tree_receive):
    hi, lo = lax.axis_index("hi"), lax.axis_index("lo")
    x, y = lo // SIDE, lo % SIDE
    z, core = hi // 2, hi % 2

    def at(dx, dy):
        return ((x + dx) % SIDE) * SIDE + (y + dy) % SIDE

    def flip(value, bit):
        return value + (1 << bit) - 2 * (((value // (1 << bit)) % 2) * (1 << bit))

    partners = [(hi, flip(lo, k)) for k in range(4)] + [(flip(hi, k), lo) for k in range(4)]
    barrier = pltpu.get_barrier_semaphore()
    greeted = [(hi, at(0, 1)), (hi, at(0, 3)), (hi, at(0, 2)), (hi, at(1, 0)), (hi, at(3, 0)), (hi, at(2, 0))] + partners[4:]
    for device in greeted:
        pl.semaphore_signal(barrier, inc=1, device_id=device, device_id_type=MESH)
    own = pltpu.make_async_copy(packet, gathered.at[pl.ds(lo * OWN, OWN)], own_sem)
    own.start()
    pl.semaphore_wait(barrier, len(greeted))

    sends = []

    def push(dx, dy, leaf, to, source=None):
        slot = at(dx, dy) * OWN + leaf
        copy = pltpu.make_async_remote_copy(
            src_ref=packet.at[leaf] if (dx, dy) == (0, 0) else gathered.at[slot],
            dst_ref=gathered.at[slot],
            send_sem=send.at[len(sends)],
            recv_sem=receive.at[slot],
            device_id=(hi, at(*to)),
            device_id_type=MESH,
        )
        copy.start()
        sends.append(copy)

    def landed(dx, dy, leaf):
        slot = at(dx, dy) * OWN + leaf
        pltpu.make_async_remote_copy(
            src_ref=gathered.at[slot],
            dst_ref=gathered.at[slot],
            send_sem=send.at[0],
            recv_sem=receive.at[slot],
            device_id=(hi, lo),
            device_id_type=MESH,
        ).wait_recv()

    def turn(first, second, half):
        return (second, first) if half == 0 else (first, second)

    tree = []

    def tree_start(k):
        copy = pltpu.make_async_remote_copy(
            src_ref=(level if k == 0 else pending.at[k, pl.ds(0, LEVELS - k)]),
            dst_ref=arrived.at[k, pl.ds(0, LEVELS - k)],
            send_sem=tree_send.at[k],
            recv_sem=tree_receive.at[k],
            device_id=partners[k],
            device_id_type=MESH,
        )
        copy.start()
        tree.append(copy)

    def tree_finish(k):
        tree[k].wait_recv()
        sibling[k] = arrived[k, 0]
        if k < LEVELS - 1:
            mine = level if k == 0 else pending.at[k]
            pending[k + 1, pl.ds(0, LEVELS - 1 - k)] = mine[pl.ds(1, LEVELS - 1 - k)] + arrived[k, pl.ds(1, LEVELS - 1 - k)]

    tree_start(0)
    for half in (0, 1):
        for leaf in (2 * half, 2 * half + 1):
            for step in (1, 3):
                push(0, 0, leaf, turn(step, 0, half) if half else (0, step))
    for half in (0, 1):
        for leaf in (2 * half, 2 * half + 1):
            for step in (1, 3):
                push(0, 0, leaf, (step, 0) if half == 0 else (0, step))
    tree_finish(0)
    tree_start(1)

    def first(half, step):
        return (0, step) if half == 0 else (step, 0)

    def second(half, step):
        return (step, 0) if half == 0 else (0, step)

    def add(a, b):
        return (a[0] + b[0], a[1] + b[1])

    for half in (0, 1):
        for leaf in (2 * half, 2 * half + 1):
            for step in (3, 1):
                landed(*first(half, step), leaf)
                if (leaf % 2 == 0) == (step == 3):
                    push(*first(half, step), leaf, first(half, 4 - step))
                push(*first(half, step), leaf, second(half, 1))
                push(*first(half, step), leaf, second(half, 3))
    tree_finish(1)
    tree_start(2)
    for half in (0, 1):
        for leaf in (2 * half, 2 * half + 1):
            for step in (3, 1):
                landed(*second(half, step), leaf)
                if (leaf % 2 == 0) == (step == 3):
                    push(*second(half, step), leaf, second(half, 4 - step))
    tree_finish(2)
    tree_start(3)
    for half in (0, 1):
        for leaf in (2 * half, 2 * half + 1):
            landed(*first(half, 2), leaf)
            push(*first(half, 2), leaf, second(half, 1))
            push(*first(half, 2), leaf, second(half, 3))
    tree_finish(3)
    tree_start(4)
    for across in (3, 1, 2):
        for half in (0, 1):
            for leaf in (2 * half, 2 * half + 1):
                for step in (3, 1):
                    where = add(first(half, across), second(half, step))
                    landed(*where, leaf)
                    if (leaf % 2 == 0) == (step == 3):
                        push(*where, leaf, second(half, 4 - step))
        if across == 3:
            tree_finish(4)
            tree_start(5)
        if across == 1:
            tree_finish(5)
            tree_start(6)
    tree_finish(6)
    tree_start(7)
    for across in (0, 3, 1, 2):
        for half in (0, 1):
            for leaf in (2 * half, 2 * half + 1):
                landed(*add(first(half, across), second(half, 2)), leaf)
    tree_finish(7)
    for copy in sends:
        copy.wait_send()
    for copy in tree:
        copy.wait_send()
    own.wait()


def exchange(packet, level):
    return pl.pallas_call(
        exchange_kernel,
        out_shape=(
            jax.ShapeDtypeStruct((GROUP, ROWS, LEAF), f32),
            jax.ShapeDtypeStruct((LEVELS, PROBES, RANK), f32),
        ),
        in_specs=[ANY, VMEM],
        out_specs=(ANY, VMEM),
        scratch_shapes=[
            pltpu.VMEM((LEVELS, LEVELS, PROBES, RANK), f32),
            pltpu.VMEM((LEVELS, LEVELS, PROBES, RANK), f32),
            pltpu.SemaphoreType.DMA((60,)),
            pltpu.SemaphoreType.DMA((GROUP,)),
            pltpu.SemaphoreType.DMA,
            pltpu.SemaphoreType.DMA((LEVELS,)),
            pltpu.SemaphoreType.DMA((LEVELS,)),
        ],
        compiler_params=pltpu.CompilerParams(collective_id=0, has_side_effects=True),
        name="exchange",
    )(packet, level)


def image_kernel(
    ids, counts, far_ids, gathered_hbm, sibling, residual, nugget, basis_hbm, transfer, coupling_hbm, coarse_down_hbm,
    image, stats,
    gathered, basis, coupling, coarse_down, sources, targets, values, total, distance0, distance1, task_leaf, task_source,
    coeff, sems,
):
    hi, lo = lax.axis_index("hi"), lax.axis_index("lo")
    copies = [
        pltpu.make_async_copy(gathered_hbm, gathered, sems.at[0]),
        pltpu.make_async_copy(coarse_down_hbm, coarse_down, sems.at[1]),
        pltpu.make_async_copy(coupling_hbm, coupling, sems.at[2]),
        pltpu.make_async_copy(basis_hbm, basis, sems.at[3]),
    ]
    for copy in copies:
        copy.start()
    total[...] = jnp.zeros_like(total)
    tasks = jnp.int32(0)
    for leaf in range(OWN):
        start = tasks

        @pl.loop(0, counts[leaf])
        def _(slot):
            task_leaf[start + slot] = leaf
            task_source[start + slot] = ids[leaf * NEAR + slot]

        tasks = tasks + counts[leaf]
    for extra in range(2):
        task_leaf[tasks + extra] = OWN
        task_source[tasks + extra] = 0

    def as_float(value):
        return value.astype(f32)

    center = (
        as_float(4 * (hi % 2) + 8 * ((hi // 8) % 2) + 2),
        as_float(4 * ((hi // 2) % 2) + 2),
        as_float(4 * ((hi // 4) % 2) + 2),
    )
    row = lax.broadcasted_iota(jnp.int32, (8, LEAF), 0)
    middle = jnp.where(row == 0, center[0], jnp.where(row == 1, center[1], center[2]))
    copies[0].wait()

    def features(leaf):
        raw = gathered[leaf, 16:24, :]
        moved = jnp.where(row < 3, (raw - middle) * point_scale, 0.0)
        square = jnp.sum(moved * moved, axis=0, keepdims=True)
        return moved, square

    def parts(value):
        high = value.astype(bf16).astype(f32)
        rest = value - high
        mid = rest.astype(bf16).astype(f32)
        return high, mid, rest - mid

    @pl.loop(0, GROUP)
    def _(leaf):
        moved, square = features(leaf)
        high, mid, low = parts(jnp.where(row == 3, square, jnp.where(row == 4, 1.0, moved)))
        sources[leaf] = jnp.concatenate([high, mid, high, mid, low, high], axis=0).astype(bf16)
        vh, vl = split(gathered[leaf, 0:16, :])
        values[leaf] = jnp.concatenate([vh, vl], axis=0)

    for leaf in range(OWN):
        moved, square = features(lo * OWN + leaf)
        high, mid, low = parts(jnp.where(row == 3, 1.0, jnp.where(row == 4, square, -2.0 * moved)))
        targets[leaf] = jnp.concatenate([high, high, mid, mid, high, low], axis=0).astype(bf16)

    def measure(task, into):
        leaf, source = task_leaf[task] % OWN, task_source[task]
        into[...] = lax.dot_general(
            sources[source], targets[leaf], (((0,), (0,)), ((), ())), preferred_element_type=f32
        )

    def apply(task, distance):
        leaf, source = task_leaf[task], task_source[task]
        value = values[source]
        part = jnp.zeros((2 * PROBES, LEAF), f32)
        for at in range(0, LEAF, 128):
            squared = jnp.maximum(distance[at : at + 128], 1e-30)
            scaled = squared * lax.rsqrt(squared)
            kernel = (scaled + log2e) * jnp.exp2(-scaled)
            kh, kl = split(kernel)
            here = value[:, at : at + 128]
            part += jnp.dot(
                jnp.concatenate([here, here], axis=1), jnp.concatenate([kh, kl], axis=0), preferred_element_type=f32
            )
        total[leaf] += part

    measure(0, distance0)

    @pl.loop(0, (tasks + 1) // 2)
    def _(pair):
        measure(2 * pair + 1, distance1)
        apply(2 * pair, distance0)
        measure(2 * pair + 2, distance0)
        apply(2 * pair + 1, distance1)

    copies[1].wait()
    down = jnp.zeros((PROBES, RANK), f32)
    for k in range(LEVELS):
        down += dot3(sibling[k] * 2.0 ** (-0.5 * k), coarse_down[k], NN)
    copies[2].wait()
    copies[3].wait()
    lane = lax.broadcasted_iota(jnp.int32, (PROBES, 128), 1)
    table = jnp.zeros((PROBES, 128), f32)
    for leaf in range(OWN):
        @pl.loop(0, FAR)
        def _(slot):
            source = far_ids[leaf * FAR + slot]
            for block in range(4):
                coeff[slot, 4 * block : 4 * block + 4, :] = gathered[source, 20:24, 128 * block : 128 * block + 128]

        local = dot3(down, transfer[leaf], NT)
        for slot in range(FAR):
            local += dot3(coeff[slot], coupling[leaf, slot], NN)
        direction = gathered[lo * OWN + leaf, 0:16, :]
        near = (total[leaf, 0:16] + total[leaf, 16:32]) * ln2 + nugget[leaf : leaf + 1, :] * direction
        whole = near + dot3(local, basis[leaf], NT)
        image[leaf] = whole
        mine = residual[leaf]
        small = whole * 0.0625
        for column, product in enumerate((mine * mine, direction * whole, mine * whole, small * small)):
            table += jnp.where(lane == column, jnp.sum(product, axis=1, keepdims=True), 0.0)
    stats[...] = table[0:8] + pltpu.roll(table[8:16], 4, 1)


def make_image(ids, counts, far_ids, gathered, sibling, residual, nugget, basis, transfer, coupling, coarse_down):
    return pl.pallas_call(
        image_kernel,
        out_shape=(jax.ShapeDtypeStruct((OWN, PROBES, LEAF), f32), jax.ShapeDtypeStruct((8, 128), f32)),
        in_specs=[SMEM, SMEM, SMEM, ANY, VMEM, VMEM, VMEM, ANY, VMEM, ANY, ANY],
        out_specs=(VMEM, VMEM),
        scratch_shapes=[
            pltpu.VMEM((GROUP, ROWS, LEAF), f32),
            pltpu.VMEM((OWN, LEAF, RANK), f32),
            pltpu.VMEM((OWN, FAR, RANK, RANK), f32),
            pltpu.VMEM((LEVELS, RANK, RANK), f32),
            pltpu.VMEM((GROUP, 48, LEAF), bf16),
            pltpu.VMEM((OWN, 48, LEAF), bf16),
            pltpu.VMEM((GROUP, 2 * PROBES, LEAF), bf16),
            pltpu.VMEM((OWN + 1, 2 * PROBES, LEAF), f32),
            pltpu.VMEM((LEAF, LEAF), f32),
            pltpu.VMEM((LEAF, LEAF), f32),
            pltpu.SMEM((OWN * NEAR + 4,), jnp.int32),
            pltpu.SMEM((OWN * NEAR + 4,), jnp.int32),
            pltpu.VMEM((FAR, PROBES, RANK), f32),
            pltpu.SemaphoreType.DMA((4,)),
        ],
        compiler_params=pltpu.CompilerParams(vmem_limit_bytes=48 * 2**20),
        name="image",
    )(ids, counts, far_ids, gathered, sibling, residual, nugget, basis, transfer, coupling, coarse_down)


def reduce_kernel(stats, scalars, middle, inner, outer, inner_send, inner_receive, outer_send, outer_receive):
    hi, lo = lax.axis_index("hi"), lax.axis_index("lo")
    barrier = pltpu.get_barrier_semaphore()
    near = [(hi, (lo + step) % PEERS) for step in range(1, PEERS)]
    far = [((hi + step) % (2 * DEPTH), lo) for step in range(1, 2 * DEPTH)]
    for device in near + far:
        pl.semaphore_signal(barrier, inc=1, device_id=device, device_id_type=MESH)
    pl.semaphore_wait(barrier, len(near) + len(far))

    def all_sum(source, slots, send, receive, devices):
        copies = []
        for index, device in enumerate(devices):
            copy = pltpu.make_async_remote_copy(
                src_ref=source,
                dst_ref=slots.at[index],
                send_sem=send.at[index],
                recv_sem=receive.at[index],
                device_id=device,
                device_id_type=MESH,
            )
            copy.start()
            copies.append(copy)
        total = source[...]
        for index, copy in enumerate(copies):
            copy.wait_recv()
            total += slots[index]
        return total, copies

    middle[...], first = all_sum(stats, inner, inner_send, inner_receive, near)
    total, second = all_sum(middle, outer, outer_send, outer_receive, far)
    table = jnp.concatenate([total, pltpu.roll(total, 124, 1)], axis=0)
    start, curvature, cross, square = (table[:, q : q + 1] for q in range(4))
    alpha = start / curvature
    finish = start - 2.0 * (alpha * cross) + (alpha * square) * alpha * 256.0
    beta = finish / (start + epsilon)
    lane = lax.broadcasted_iota(jnp.int32, (PROBES, 128), 1)
    scalars[...] = jnp.where(lane == 0, alpha, beta)
    for copy in first + second:
        copy.wait_send()


def reduce_all(stats):
    return pl.pallas_call(
        reduce_kernel,
        out_shape=jax.ShapeDtypeStruct((PROBES, 128), f32),
        in_specs=[VMEM],
        out_specs=VMEM,
        scratch_shapes=[
            pltpu.VMEM((8, 128), f32),
            pltpu.VMEM((PEERS - 1, 8, 128), f32),
            pltpu.VMEM((2 * DEPTH - 1, 8, 128), f32),
            pltpu.SemaphoreType.DMA((PEERS - 1,)),
            pltpu.SemaphoreType.DMA((PEERS - 1,)),
            pltpu.SemaphoreType.DMA((2 * DEPTH - 1,)),
            pltpu.SemaphoreType.DMA((2 * DEPTH - 1,)),
        ],
        compiler_params=pltpu.CompilerParams(collective_id=1, has_side_effects=True),
        name="reduce",
    )(stats)


def per_device(
    points, solution, residual, direction, nugget, leaf_basis, transfer, far_coupling, coarse_up, coarse_down,
    near_ids, near_count, far_ids,
):
    group_start = lax.axis_index("hi") * GROUP
    by_leaf = jnp.swapaxes(direction, 0, 1)
    high = lax.Precision.HIGHEST
    coefficients = jnp.einsum("lna,lar->lnr", by_leaf, leaf_basis, precision=high)
    box = jnp.einsum("lnq,lqr->nr", coefficients, transfer, precision=high)
    level = jnp.einsum("nq,kqr->knr", box, coarse_up[0], precision=high)
    coeff_rows = coefficients.reshape(OWN, 4, 4, RANK).swapaxes(1, 2).reshape(OWN, 4, LEAF)
    packet = jnp.concatenate(
        [by_leaf, jnp.swapaxes(points, 0, 1), jnp.zeros((OWN, 1, LEAF), f32), coeff_rows], axis=1
    )
    gathered, sibling = exchange(packet, level)
    image, stats = make_image(
        (near_ids - group_start).reshape(-1), near_count, (far_ids - group_start).reshape(-1),
        gathered, sibling, jnp.swapaxes(residual, 0, 1), nugget, leaf_basis, transfer, far_coupling, coarse_down[0],
    )
    scalars = reduce_all(stats)
    alpha, beta = scalars[:, 0:1, None], scalars[:, 1:2, None]
    new_solution = solution + alpha * direction
    new_residual = residual - alpha * jnp.swapaxes(image, 0, 1)
    return new_solution, new_residual, new_residual + beta * direction


def solution(mesh):
    vector, leaf = P(None, ("hi", "lo"), None), ("hi", "lo")
    return jax.shard_map(
        per_device,
        mesh=mesh,
        in_specs=(
            vector, vector, vector, vector, P(leaf, None), P(leaf, None, None), P(leaf, None, None),
            P(leaf, None, None, None), P(leaf, None, None, None), P(leaf, None, None, None),
            P(leaf, None), P(leaf), P(leaf, None),
        ),
        out_specs=(vector, vector, vector),
        check_vma=False,
    )
```

time: 541 us -> 131 us (0.24)
  blocking collectives: 342 us -> 0 us
  Pallas kernels: 0 us -> 111 us
  matrix products: 91.1 us -> 4.22 us
  local copies, waits for them, and re-layouts: 40.4 us -> 12 us
  starting transfers between devices: 25.8 us -> 0 us
  between operations: 14.3 us -> 0.77 us
  waiting for transfers between devices: 12.4 us -> 0 us
  loops' own time: 9.41 us -> 0 us
    psum x2 -> x0, blocking collectives: 306 us -> none  [the longest x1 231 us: per_device(): start = lax.psum(local_square, ('hi', 'lo'))]
    pallas_call x0 -> x3, Pallas kernels: none -> 111 us  [the longest x1 44 us: reduce_all(): pl.pallas_call(reduce_kernel, out_shape=jax.ShapeDtypeStruct((PROBES, 128...]
    dot_general x19 -> x3, matrix products: 91.1 us -> 4.22 us  [the longest x1 2.04 us: per_device(): jnp.einsum('lna,lar->lnr', by_leaf, leaf_basis, precision=high)]
    all_gather x2 -> x0, blocking collectives: 36.7 us -> none  [the longest x1 19.4 us: per_device(): lax.all_gather(coefficients, 'lo', axis=1, tiled=True)]
    gather x25 -> x0, local copies, waits for them, and re-layouts: 33.3 us -> none  [the longest x12 25.7 us: block_product(): values = jnp.take(group_values, source_leaves, axis=1)]
    ppermute x8 -> x0, starting transfers between devices: 25.8 us -> none  [partner(): lax.ppermute(array, axis, [(i, i ^ 1 << apart) for i in range(lax.axis_si...]
    ppermute x8 -> x0, waiting for transfers between devices: 12.3 us -> none  [partner(): lax.ppermute(array, axis, [(i, i ^ 1 << apart) for i in range(lax.axis_si...]
    another operation x1 -> x0, loops' own time: 9.41 us -> none  [per_device(): lax.fori_loop(0, turns, near_turn, jnp.zeros((probe_count, leaf_count, le...]
  transfers between devices with their start and end apart: 9 -> 0, of which waited for: 6 -> 0; matrix products, arithmetic and copies ran while one was open for 2% -> 0% of each run, Pallas kernels for 0% -> 0%
where the time goes in v1:
time: 131 us; the launch traced here: 132 us
  Pallas kernels  111 us (85%)
  local copies, waits for them, and re-layouts  12 us (9%)
  matrix products  4.22 us (3%)
  other arithmetic  3 us (2%)
    pallas_call x1, Pallas kernels, reduce_all(): pl.pallas_call(reduce_kernel, out_shape=jax.ShapeDtypeStruct((PROBES, 128...  44 us
    pallas_call x1, Pallas kernels, exchange(): pl.pallas_call(exchange_kernel, out_shape=(jax.ShapeDtypeStruct((GROUP, R...  39.8 us
    pallas_call x1, Pallas kernels, make_image(): pl.pallas_call(image_kernel, out_shape=(jax.ShapeDtypeStruct((OWN, PROBES...  27.6 us
    unnamed x29, local copies, waits for them, and re-layouts  10.8 us

profile of v1, /device:TPU:1, one launch (start us, length us, event | category | flops | bytes accessed | tf_op | source)
XLA Modules:
  0.0 131.5 jit_solution(880773207282886408)
XLA Ops:
  0.6 0.0 copy-start
  0.6 0.0 copy-start.1
  0.7 2.0 %fusion.1 = f32[4,16,128]{2,1,0:T(8,128)S(1)} fusion(f32[4,512,128]{2,1,0:T(8,128)} %basis_hbm.1, f32[16,4,512]{2,1,0:T(4,128)} %param.16), kind=kOutput, calls=%fused_computation.14 | convolution fusion | flops 50331648 | bytes 1212416 | tf_op jit(solution)/shard_map/lna,lar->lnr/dot_general | solution.py:430
  2.7 1.0 copy.41
  3.7 0.8 copy.43
  4.5 0.1 pad.2.clone
  4.5 0.8 pad_maximum_fusion.packet
  5.3 1.2 fusion.2
  6.5 0.0 copy-done
  6.5 1.0 convolution_bitcast_fusion.level
  7.5 39.8 %exchange.1 = (f32[64,24,512]{2,1,0:T(8,128)}, f32[8,16,128]{2,1,0:T(8,128)}) custom-call(f32[4,24,512]{2,1,0:T(8,128)} %pad_maximum_fusion.packet, f32[8,16,128]{2,1,0:T(8,128)} %convolution_bitcast_fusion.level), custom_call_target="tpu_custom_call" | custom-call | tf_op jit(solution)/shard_map/exchange/pallas_call | solution.py:187
  47.4 0.7 broadcast_subtract_fusion.1
  48.1 0.1 reshape.20.ids
  48.1 0.7 broadcast_subtract_fusion
  48.8 0.1 reshape.21.far_ids
  48.9 0.9 copy.40
  49.9 0.0 copy-done.1
  49.9 0.0 copy-start.2
  49.9 1.9 %copy-done.2 = f32[64,24,512]{2,1,0:T(8,128)S(1)} copy-done((f32[64,24,512]{2,1,0:T(8,128)S(1)}, f32[64,24,512]{2,1,0:T(8,128)}, u32[]{:S(2)}) %copy-start.2) | copy-done | bytes 3145752
  51.8 0.0 copy-start.3
  51.8 0.9 copy-done.3
  52.7 0.0 copy-start.4
  52.7 1.0 copy-done.4
  53.8 0.0 copy-start.5
  53.8 0.8 copy-done.5
  54.6 0.0 copy-start.6
  54.6 0.7 copy-done.6
  55.3 0.0 copy-start.8
  55.3 0.7 copy-done.8
  55.9 0.0 copy-start.9
  56.0 0.0 copy-start.10
  56.0 0.0 copy-start.11
  56.0 27.6 %image.1 = (f32[4,16,512]{2,1,0:T(8,128)S(1)}, f32[8,128]{1,0:T(8,128)S(1)}) custom-call(s32[108]{0:T(128)S(1)} %reshape.20.ids, s32[4]{0:T(128)S(1)} %copy-done.8, s32[64]{0:T(128)S(1)} %reshape.21.far_ids, f32[64,24,512]{2,1,0:T(8,128)S(1)} %copy-done.2, f32[8,16,128]{2,1,0:T(8,128)S(1)} %copy-done.5, f32[4,16,512]{2,1,0:T(8,128)S(1)} %bitcast.29, ...), custom_call_target="tpu_custom_call" | custom-call | tf_op jit(solution)/shard_map/image/pallas_call | solution.py:336
  83.6 0.0 copy-start.7
  83.6 0.6 copy-done.7
  84.2 44.0 %reduce.5 = f32[16,128]{1,0:T(8,128)} custom-call(f32[8,128]{1,0:T(8,128)} %copy-done.7), custom_call_target="tpu_custom_call" | custom-call | tf_op jit(solution)/shard_map/reduce/pallas_call | solution.py:404
  128.2 1.0 slice_reduce_fusion
  129.1 0.0 copy-done.9
  129.1 0.0 copy-done.10
  129.2 0.1 multiply_add_fusion
  129.3 0.7 copy.30
  130.0 0.7 copy.31
  130.8 0.0 copy-done.11
  130.8 0.8 multiply_add_fusion.1
  (2 shorter events, 0.0 us)
Async XLA Ops:
  0.6 5.9 %copy-start = (f32[1,8,128,128]{3,2,1,0:T(8,128)S(1)}, f32[1,8,128,128]{3,2,1,0:T(8,128)}, u32[]{:S(2)}) copy-start(f32[1,8,128,128]{3,2,1,0:T(8,128)} %param.21) | copy-start | bytes 1572868
  0.6 49.2 %copy-start.1 = (f32[4,512,128]{2,1,0:T(8,128)S(1)}, f32[4,512,128]{2,1,0:T(8,128)}, u32[]{:S(2)}) copy-start(f32[4,512,128]{2,1,0:T(8,128)} %basis_hbm.1) | copy-start | bytes 3145732
  49.9 1.9 %copy-start.2 = (f32[64,24,512]{2,1,0:T(8,128)S(1)}, f32[64,24,512]{2,1,0:T(8,128)}, u32[]{:S(2)}) copy-start(f32[64,24,512]{2,1,0:T(8,128)} %get-tuple-element.7.gathered_hbm) | copy-start | bytes 9437188
  51.8 0.9 copy-start.3
  52.7 1.0 copy-start.4
  53.8 0.8 copy-start.5
  54.6 0.7 copy-start.6
  55.3 0.7 copy-start.8
  55.9 73.2 %copy-start.9 = (f32[16,4,512]{2,1,0:T(4,128)S(1)}, f32[16,4,512]{2,1,0:T(4,128)}, u32[]{:S(2)}) copy-start(f32[16,4,512]{2,1,0:T(4,128)} %param.16) | copy-start | bytes 393220
  56.0 73.2 %copy-start.10 = (f32[16,4,512]{2,1,0:T(4,128)S(1)}, f32[16,4,512]{2,1,0:T(4,128)}, u32[]{:S(2)}) copy-start(f32[16,4,512]{2,1,0:T(4,128)} %param.15) | copy-start | bytes 393220
  56.0 74.8 %copy-start.11 = (f32[16,4,512]{2,1,0:T(4,128)S(1)}, f32[16,4,512]{2,1,0:T(4,128)}, u32[]{:S(2)}) copy-start(f32[16,4,512]{2,1,0:T(4,128)} %param.14) | copy-start | bytes 393220
  83.6 0.6 copy-start.7
